TPU v7x, 512 devices: a whole 4x8x8 slice. The times are simulated.
512 devices in a mesh: dom: 128 (over y, z, core), scen: 4 (over x).
Axes of the slice: x: 4, y: 8, z: 8, core: 2. Of those that a mesh axis runs over, the one named last changes fastest.
Arguments:
- embedding: bfloat16 [1310720, 256], P(('dom', 'scen')), may hold values from -6 to 6
- scenario_feats: bfloat16 [16, 1310720], P(None, ('dom', 'scen')), may hold values from -6 to 6
- adjacency: bfloat16 [10240, 2, 128, 128], P(('dom', 'scen')), may hold values from -0.3125 to 0.3125
- driver_weight: bfloat16 [1310720, 128], P(('dom', 'scen')), may hold values from -0.3125 to 0.3125
- local_slot: int32 [10240], P(('dom', 'scen')), may hold values from 0 to 79, as said below
- halo_slot: int32 [10240], P(('dom', 'scen')), may hold values from 0 to 15, as said below
- send_rows: int32 [65536, 16], P(('dom', 'scen')), may hold values from 0 to 2559
- send_count: int32 [65536], P(('dom', 'scen')), may hold values from 1 to 16, as said below
- hot_ids: int32 [128], replicated, may hold values from 0 to 1310719, as said below
- first_weight: bfloat16 [512, 256], P('scen'), may hold values from -0.25 to 0.25
- feature_weight: bfloat16 [16, 256], replicated, may hold values from -1.5 to 1.5
- first_bias: float32 [256], replicated, may hold values from -3 to 3
- second_weight: bfloat16 [256, 256], P('scen'), may hold values from -0.375 to 0.375
- second_bias: float32 [256], replicated, may hold values from -3 to 3
Outputs:
- updated: bfloat16 [1310720, 256], P(('dom', 'scen'))
Inputs may be any that keep to these rules, and one draw needn't show every extreme that they name: `local_slot`: the 20 entries of one device are distinct and name exactly 5 tiles of each device of its partition; values s * 20 to s * 20 + 19 are tiles of scen index s. `halo_slot`: the entries of one device name every halo tile at least once. `send_count`: every device has a partition to which it sends 16 pins. `hot_ids`: no device holds more than 1 of them, and some device holds exactly that many.
All inputs are finite; a program needn't handle non-finite values.
Results may differ from a plain program's by a relative error of at most 0.0038.
Values may be sent and summed in bfloat16 or wider, within the bound.
No kernel may reach another device: no remote copies, remote signals or barrier semaphores. Data moves between devices by JAX's collectives and lax.ppermute only.
A program may use at most 64 MiB of HBM per device.

v0:
```python
import jax
import jax.numpy as jnp
from jax import lax
from jax.sharding import PartitionSpec as P


def per_device(
    embedding,
    scenario_feats,
    adjacency,
    driver_weight,
    local_slot,
    halo_slot,
    send_rows,
    send_count,
    hot_ids,
    first_weight,
    feature_weight,
    first_bias,
    second_weight,
    second_bias,
):
    rows, width = embedding.shape
    tile = adjacency.shape[-1]
    tiles = rows // tile
    groups = lax.axis_size("scen")
    partition = lax.all_gather(embedding, "scen", axis=0, tiled=True)
    local_tiles = partition.reshape(groups * tiles, tile, width)[local_slot]
    slots_per_peer = send_rows.shape[1]
    live = jnp.arange(slots_per_peer, dtype=jnp.int32)[None, :] < send_count[:, None]
    outgoing_rows = jnp.where(
        live[:, :, None], embedding[send_rows], jnp.zeros((), embedding.dtype)
    )
    incoming = lax.all_to_all(outgoing_rows, "dom", split_axis=0, concat_axis=0, tiled=True)
    halo_tiles = incoming.reshape(-1, tile, width)[halo_slot]
    myself = lax.axis_index(("dom", "scen"))
    owner = hot_ids // rows
    within = hot_ids - owner * rows
    mine = jnp.where(
        (owner == myself)[:, None], embedding[within].astype(jnp.float32), jnp.float32(0.0)
    )
    drivers = lax.psum(mine, ("dom", "scen")).astype(jnp.bfloat16)
    summed = jnp.einsum(
        "tij,tjc->tic", adjacency[:, 0], local_tiles, preferred_element_type=jnp.float32
    )
    summed = summed + jnp.einsum(
        "tij,tjc->tic", adjacency[:, 1], halo_tiles, preferred_element_type=jnp.float32
    )
    summed = summed.reshape(rows, width) + jnp.dot(
        driver_weight, drivers, preferred_element_type=jnp.float32
    )
    aggregate = summed.astype(jnp.bfloat16)
    joined = jnp.concatenate([embedding, aggregate], axis=1)
    starting = (
        jnp.dot(scenario_feats.T, feature_weight, preferred_element_type=jnp.float32) + first_bias
    )
    columns = joined
    inner = starting + jnp.dot(
        columns,
        lax.all_gather(first_weight, "scen", axis=0, tiled=True),
        preferred_element_type=jnp.float32,
    )
    activated = jax.nn.gelu(inner, approximate=False).astype(jnp.bfloat16)
    residual = embedding.astype(jnp.float32) + second_bias
    columns = activated
    result = residual + jnp.dot(
        columns,
        lax.all_gather(second_weight, "scen", axis=0, tiled=True),
        preferred_element_type=jnp.float32,
    )
    return result.astype(jnp.bfloat16)


def solution(mesh):
    return jax.shard_map(
        per_device,
        mesh=mesh,
        in_specs=(
            P(("dom", "scen"), None),
            P(None, ("dom", "scen")),
            P(("dom", "scen"), None, None, None),
            P(("dom", "scen"), None),
            P(("dom", "scen")),
            P(("dom", "scen")),
            P(("dom", "scen"), None),
            P(("dom", "scen")),
            P(),
            P("scen", None),
            P(),
            P(),
            P("scen", None),
            P(),
        ),
        out_specs=P(("dom", "scen"), None),
        check_vma=False,
    )
```

profile of v0, /device:TPU:8, one launch (start us, length us, event | category | flops | bytes accessed | tf_op | source)
XLA Modules:
  0.0 204.4 jit_solution(11013594092646320890)
XLA Ops:
  6.5 0.7 all-gather.2.cloned.1.call-update
  7.3 0.7 compare_select_fusion
  8.0 0.1 copy.18
  8.1 0.1 reshape.46
  8.2 0.0 copy-start.6
  8.2 7.5 %gather_fusion.1 = bf16[2048,256]{1,0:T(8,128)(2,1)S(1)} fusion(bf16[2560,256]{1,0:T(8,128)(2,1)S(1)} %copy-done.1, s32[2048]{0:T(1024)S(1)} %broadcast_clamp_fusion), kind=kCustom, calls=%fused_computation.1 | custom fusion | bytes 2105344 | tf_op jit(solution)/shard_map/gather | solution.py:32
  15.7 0.0 copy-start.7
  15.7 0.1 iota_compare_fusion
  15.8 0.0 copy-start.5
  15.8 0.0 copy-start.4
  15.8 1.2 broadcast_select_fusion
  17.1 17.4 %all-to-all-start = ((bf16[128,16,256]{2,1,0:T(8,128)(2,1)}), bf16[128,16,256]{2,1,0:T(8,128)(2,1)S(1)}, u32[]{:S(2)}, u32[]{:S(2)}) async-start(bf16[128,16,256]{2,1,0:T(8,128)(2,1)} %broadcast_select_fusion), calls=%async_computation | async-start | bytes 2097152 | tf_op jit(solution)/shard_map/all_to_all | solution.py:34
  34.5 0.8 gather_fusion.3
  35.3 0.1 convert_select_fusion
  35.4 114.3 %all-reduce.1 = bf16[128,256]{1,0:T(8,128)(2,1)S(1)} all-reduce(f32[128,256]{1,0:T(8,128)S(1)} %convert_select_fusion), channel_id=1, replica_groups=mesh['dom'=128,'scen'=4] {'dom','scen'}, use_global_device_ids=true, to_apply=%region_0.1 | all-reduce | flops 32768 | bytes 196608 | tf_op jit(solution)/shard_map/psum | solution.py:42
  149.8 12.2 %all_gather.11 = bf16[256,256]{1,0:T(8,128)(2,1)S(1)} all-gather(bf16[64,256]{1,0:T(8,128)(2,1)} %param.26), channel_id=1, replica_groups=mesh['dom'=128,'scen'=4] {'scen'}, dimensions={0}, use_global_device_ids=true | all-gather | bytes 163840 | tf_op jit(solution)/shard_map/all_gather | solution.py:68
  162.0 13.2 %all_gather.10 = bf16[512,256]{1,0:T(8,128)(2,1)} all-gather(bf16[128,256]{1,0:T(8,128)(2,1)S(1)} %copy-done.5), channel_id=1, replica_groups=mesh['dom'=128,'scen'=4] {'scen'}, dimensions={0}, use_global_device_ids=true | all-gather | bytes 327680 | tf_op jit(solution)/shard_map/all_gather | solution.py:60
  175.1 0.7 compare_select_fusion.2
  175.8 0.7 compare_select_fusion.3
  176.4 0.6 pad_clamp_fusion.2
  177.0 2.7 %convolution_add_fusion.2 = f32[2560,256]{1,0:T(8,128)} fusion(bf16[16,2560]{1,0:T(8,128)(2,1)S(1)} %copy-done.4, bf16[16,256]{1,0:T(8,128)(2,1)} %param.24, f32[256]{0:T(256)} %param.25), kind=kOutput, calls=%fused_computation.6 | convolution fusion | flops 21626880 | bytes 2712576 | tf_op jit(solution)/shard_map/dot_general | solution.py:55
  179.8 1.8 gather_fusion.2
  181.5 3.2 %gather_fusion = bf16[20,128,256]{2,1,0:T(8,128)(2,1)S(1)} fusion(bf16[80,128,256]{2,1,0:T(8,128)(2,1)} %bitcast.33, s32[1024]{0:T(1024)} %pad_clamp_fusion.2), kind=kCustom, calls=%fused_computation | custom fusion | bytes 2621520 | tf_op jit(solution)/shard_map/gather | solution.py:28
  184.8 0.0 copy-start.2
  184.8 0.0 copy-start.3
  184.8 1.7 fusion.52
  186.6 0.1 copy-done.3
  186.7 0.5 convolution_add_fusion.3
  187.2 0.0 copy-start.8
  187.2 0.5 fusion.1
  187.7 0.2 copy-done.8
  187.9 9.7 %fusion.2 = bf16[2560,256]{1,0:T(8,128)(2,1)} fusion(bf16[256,256]{1,0:T(8,128)(2,1)S(1)} %all_gather.11, bf16[2560,256]{1,0:T(8,128)(2,1)S(1)} %copy-done.1, f32[256]{0:T(256)S(1)} %copy-done.8, f32[2560,256]{1,0:T(8,128)} %convolution_add_fusion.2, bf16[512,256]{1,0:T(8,128)(2,1)} %all_gather.10, bf16[2560,256]{1,0:T(8,128)(2,1)S(1)} %fusion.1), kind=kOutput, calls=%fused_computation.11 | convolution fusion | flops 1057751040 | bytes 6947840 | tf_op jit(solution)/shard_map/dot_general | solution.py:66
  (17 shorter events, 0.1 us)
Async XLA Ops:
  6.5 180.7 %copy-start = (bf16[2560,128]{1,0:T(8,128)(2,1)S(1)}, bf16[2560,128]{1,0:T(8,128)(2,1)}, u32[]{:S(2)}) copy-start(bf16[2560,128]{1,0:T(8,128)(2,1)} %param.17) | copy-start | bytes 1966084
  6.5 1.6 copy-start.1
  6.5 175.0 %all-gather.2.cloned.1.call-start = ((), (), s32[]{:S(2)}) async-start(), calls=%async_computation.1 | async-start | bytes 6553600 | tf_op jit(solution)/shard_map/all_gather | solution.py:27
  8.2 7.5 %copy-start.6 = (s32[128]{0:T(128)S(1)}, s32[128]{0:T(128)}, u32[]{:S(2)}) copy-start(s32[128]{0:T(128)} %param.21) | copy-start | bytes 1540
  15.7 18.8 %copy-start.7 = (s32[128]{0:T(128)S(1)}, s32[128]{0:T(128)}, u32[]{:S(2)}) copy-start(s32[128]{0:T(128)} %param.22) | copy-start | bytes 1540
  15.8 146.2 %copy-start.5 = (bf16[128,256]{1,0:T(8,128)(2,1)S(1)}, bf16[128,256]{1,0:T(8,128)(2,1)}, u32[]{:S(2)}) copy-start(bf16[128,256]{1,0:T(8,128)(2,1)} %param.23) | copy-start | bytes 196612
  15.8 161.2 %copy-start.4 = (bf16[16,2560]{1,0:T(8,128)(2,1)S(1)}, bf16[16,2560]{1,0:T(8,128)(2,1)}, u32[]{:S(2)}) copy-start(bf16[16,2560]{1,0:T(8,128)(2,1)} %param.15) | copy-start | bytes 245764
  17.1 162.7 %all-to-all-start = ((bf16[128,16,256]{2,1,0:T(8,128)(2,1)}), bf16[128,16,256]{2,1,0:T(8,128)(2,1)S(1)}, u32[]{:S(2)}, u32[]{:S(2)}) async-start(bf16[128,16,256]{2,1,0:T(8,128)(2,1)} %broadcast_select_fusion), calls=%async_computation | async-start | bytes 2097152 | tf_op jit(solution)/shard_map/all_to_all | solution.py:34
  184.8 1.8 copy-start.2
  184.8 1.9 copy-start.3
  187.2 0.7 copy-start.8
Sparse Core Ops, SparseCore 0:
  9.5 66.8 all-gather.1
where the time goes:
time: 205 us; the launch traced here: 204 us
  blocking collectives  140 us (68%)
  starting transfers between devices  17.4 us (8%)
  matrix products  15.1 us (7%)
  local copies, waits for them, and re-layouts  13.9 us (7%)
  between operations  13.6 us (7%)
  other arithmetic  4.05 us (2%)
    psum x1, blocking collectives, per_device(): drivers = lax.psum(mine, ('dom', 'scen')).astype(jnp.bfloat16)  114 us
    all_to_all x1, starting transfers between devices, per_device(): lax.all_to_all(outgoing_rows, 'dom', split_axis=0, concat_axis=0, tiled=T...  17.4 us
    all_gather x1, blocking collectives, per_device(): lax.all_gather(first_weight, 'scen', axis=0, tiled=True)  13.2 us
    all_gather x1, blocking collectives, per_device(): lax.all_gather(second_weight, 'scen', axis=0, tiled=True)  12.2 us
    dot_general x1, matrix products, per_device(): jnp.dot(columns, lax.all_gather(second_weight, 'scen', axis=0, tiled=True...  9.68 us
    gather x1, local copies, waits for them, and re-layouts, per_device(): embedding[send_rows]  7.5 us
  transfers between devices with their start and end apart: 2, of which 0 were waited for; matrix products, arithmetic and copies ran while one was open for 8% of the time, Pallas kernels for 0%

commit v1 on v0

--- a/solution.py
+++ b/solution.py
@@ -39,7 +39,7 @@
     mine = jnp.where(
         (owner == myself)[:, None], embedding[within].astype(jnp.float32), jnp.float32(0.0)
     )
-    drivers = lax.psum(mine, ("dom", "scen")).astype(jnp.bfloat16)
+    drivers = lax.psum(lax.psum(mine, "dom"), "scen").astype(jnp.bfloat16)
     summed = jnp.einsum(
         "tij,tjc->tic", adjacency[:, 0], local_tiles, preferred_element_type=jnp.float32
     )

time: 205 us -> 258 us (1.26)
  the two profiles are of different devices: /device:TPU:8 before, /device:TPU:16 now
where the time goes in v1:
time: 258 us; the launch traced here: 257 us
  waiting for transfers between devices  145 us (56%)
  blocking collectives  46 us (18%)
  starting transfers between devices  17.4 us (7%)
  local copies, waits for them, and re-layouts  15.2 us (6%)
  between operations  15.1 us (6%)
  matrix products  14.4 us (6%)
  other arithmetic  4.28 us (2%)
    psum x1, waiting for transfers between devices, per_device(): drivers = lax.psum(lax.psum(mine, 'dom'), 'scen').astype(jnp.bfloat16)  145 us
    psum x1, blocking collectives, per_device(): drivers = lax.psum(lax.psum(mine, 'dom'), 'scen').astype(jnp.bfloat16)  19.2 us
    all_to_all x1, starting transfers between devices, per_device(): lax.all_to_all(outgoing_rows, 'dom', split_axis=0, concat_axis=0, tiled=T...  17.3 us
    all_gather x1, blocking collectives, per_device(): lax.all_gather(first_weight, 'scen', axis=0, tiled=True)  14 us
    all_gather x1, blocking collectives, per_device(): lax.all_gather(second_weight, 'scen', axis=0, tiled=True)  12.8 us
    dot_general x1, matrix products, per_device(): jnp.dot(columns, lax.all_gather(second_weight, 'scen', axis=0, tiled=True...  9.68 us
    gather x1, local copies, waits for them, and re-layouts, per_device(): embedding[send_rows]  7.5 us
  transfers between devices with their start and end apart: 3, of which 1 were waited for; matrix products, arithmetic and copies ran while one was open for 5% of the time, Pallas kernels for 0%

profile of v1, /device:TPU:16, one launch (start us, length us, event | category | flops | bytes accessed | tf_op | source)
XLA Modules:
  0.0 257.4 jit_solution(3085792386285247809)
XLA Ops:
  7.4 0.8 broadcast_compare_fusion
  8.2 0.7 compare_select_fusion.1
  8.9 2.2 gather_fusion.3
  11.1 0.8 convert_select_fusion
  11.9 0.0 all-reduce.3.cloned.1.call-update
  11.9 0.0 all-gather.2.cloned.1.call-start
  11.9 0.5 all-gather.2.cloned.1.call-update
  12.5 0.7 compare_select_fusion
  13.2 0.1 copy.18
  13.3 0.1 reshape.46
  13.4 7.5 %gather_fusion.1 = bf16[2048,256]{1,0:T(8,128)(2,1)S(1)} fusion(bf16[2560,256]{1,0:T(8,128)(2,1)S(1)} %copy-done.1, s32[2048]{0:T(1024)S(1)} %broadcast_clamp_fusion), kind=kCustom, calls=%fused_computation.1 | custom fusion | bytes 2105344 | tf_op jit(solution)/shard_map/gather | solution.py:32
  20.9 0.0 copy-start.6
  20.9 0.0 copy-start.12
  20.9 0.0 copy-start.4
  21.0 0.0 copy-start.8
  21.0 0.1 iota_compare_fusion
  21.1 1.2 broadcast_select_fusion
  22.3 17.3 %all-to-all-start = ((bf16[128,16,256]{2,1,0:T(8,128)(2,1)}), bf16[128,16,256]{2,1,0:T(8,128)(2,1)S(1)}, u32[]{:S(2)}, u32[]{:S(2)}) async-start(bf16[128,16,256]{2,1,0:T(8,128)(2,1)} %broadcast_select_fusion), calls=%async_computation | async-start | bytes 2097152 | tf_op jit(solution)/shard_map/all_to_all | solution.py:34
  39.7 12.8 %all_gather.11 = bf16[256,256]{1,0:T(8,128)(2,1)S(1)} all-gather(bf16[64,256]{1,0:T(8,128)(2,1)S(1)} %copy-done.6), channel_id=1, replica_groups=mesh['dom'=128,'scen'=4] {'scen'}, dimensions={0}, use_global_device_ids=true | all-gather | bytes 163840 | tf_op jit(solution)/shard_map/all_gather | solution.py:68
  52.5 14.0 %all_gather.10 = bf16[512,256]{1,0:T(8,128)(2,1)} all-gather(bf16[128,256]{1,0:T(8,128)(2,1)S(1)} %copy-done.5), channel_id=1, replica_groups=mesh['dom'=128,'scen'=4] {'scen'}, dimensions={0}, use_global_device_ids=true | all-gather | bytes 327680 | tf_op jit(solution)/shard_map/all_gather | solution.py:60
  66.6 2.0 convolution_add_fusion.2
  68.6 144.5 %all-reduce.3.cloned.1.call-done = f32[128,256]{1,0:T(8,128)} async-done(((f32[128,256]{1,0:T(8,128)}), f32[128,256]{1,0:T(8,128)}) %all-reduce.3.cloned.1.call-update) | async-done | bytes 131088 | tf_op jit(solution)/shard_map/psum | solution.py:42
  213.1 19.2 %all-reduce.4 = bf16[128,256]{1,0:T(8,128)(2,1)S(1)} all-reduce(f32[128,256]{1,0:T(8,128)} %all-reduce.3.cloned.1.call-done), channel_id=1, replica_groups=mesh['dom'=128,'scen'=4] {'scen'}, use_global_device_ids=true, to_apply=%region_1.2 | all-reduce | flops 32768 | bytes 196608 | tf_op jit(solution)/shard_map/psum | solution.py:42
  232.3 1.8 gather_fusion.2
  234.1 3.1 %gather_fusion = bf16[20,128,256]{2,1,0:T(8,128)(2,1)S(1)} fusion(bf16[80,128,256]{2,1,0:T(8,128)(2,1)} %bitcast.33, s32[1024]{0:T(1024)S(1)} %pad_clamp_fusion.2), kind=kCustom, calls=%fused_computation | custom fusion | bytes 2621520 | tf_op jit(solution)/shard_map/gather | solution.py:28
  237.2 0.0 copy-start.2
  237.2 1.7 fusion.52
  239.0 0.1 copy-done.3
  239.1 0.5 convolution_add_fusion.3
  239.7 0.5 fusion.1
  240.2 0.2 copy-done.10
  240.3 9.7 %fusion.2 = bf16[2560,256]{1,0:T(8,128)(2,1)} fusion(bf16[256,256]{1,0:T(8,128)(2,1)S(1)} %all_gather.11, bf16[2560,256]{1,0:T(8,128)(2,1)S(1)} %copy-done.1, f32[256]{0:T(256)S(1)} %copy-done.10, f32[2560,256]{1,0:T(8,128)} %convolution_add_fusion.2, bf16[512,256]{1,0:T(8,128)(2,1)} %all_gather.10, bf16[2560,256]{1,0:T(8,128)(2,1)S(1)} %fusion.1), kind=kOutput, calls=%fused_computation.11 | convolution fusion | flops 1057751040 | bytes 6947840 | tf_op jit(solution)/shard_map/dot_general | solution.py:66
  (28 shorter events, 0.1 us)
Async XLA Ops:
  7.4 232.3 %copy-start = (bf16[2560,128]{1,0:T(8,128)(2,1)S(1)}, bf16[2560,128]{1,0:T(8,128)(2,1)}, u32[]{:S(2)}) copy-start(bf16[2560,128]{1,0:T(8,128)(2,1)} %param.17) | copy-start | bytes 1966084
  7.4 6.0 %copy-start.1 = (bf16[2560,256]{1,0:T(8,128)(2,1)S(1)}, bf16[2560,256]{1,0:T(8,128)(2,1)}, u32[]{:S(2)}) copy-start(bf16[2560,256]{1,0:T(8,128)(2,1)} %param.14) | copy-start | bytes 3932164
  7.4 205.7 %all-reduce.3.cloned.1.call-start = ((), (), s32[]{:S(2)}) async-start(), calls=%async_computation.2 | async-start | bytes 262144 | tf_op jit(solution)/shard_map/psum | solution.py:42
  11.9 222.2 %all-gather.2.cloned.1.call-start = ((), (), s32[]{:S(2)}) async-start(), calls=%async_computation.1 | async-start | bytes 6553600 | tf_op jit(solution)/shard_map/all_gather | solution.py:27
  13.4 7.5 %copy-start.9 = (s32[128]{0:T(128)S(1)}, s32[128]{0:T(128)}, u32[]{:S(2)}) copy-start(s32[128]{0:T(128)} %param.21) | copy-start | bytes 1540
  20.9 18.8 %copy-start.6 = (bf16[64,256]{1,0:T(8,128)(2,1)S(1)}, bf16[64,256]{1,0:T(8,128)(2,1)}, u32[]{:S(2)}) copy-start(bf16[64,256]{1,0:T(8,128)(2,1)} %param.26) | copy-start | bytes 98308
  20.9 31.6 %copy-start.5 = (bf16[128,256]{1,0:T(8,128)(2,1)S(1)}, bf16[128,256]{1,0:T(8,128)(2,1)}, u32[]{:S(2)}) copy-start(bf16[128,256]{1,0:T(8,128)(2,1)} %param.23) | copy-start | bytes 196612
  20.9 45.6 %copy-start.11 = (s32[20]{0:T(128)S(1)}, s32[20]{0:T(128)}, u32[]{:S(2)}) copy-start(s32[20]{0:T(128)} %param.19) | copy-start | bytes 244
  20.9 45.6 %copy-start.12 = (s32[20]{0:T(128)S(1)}, s32[20]{0:T(128)}, u32[]{:S(2)}) copy-start(s32[20]{0:T(128)} %param.18) | copy-start | bytes 244
  20.9 45.6 %copy-start.4 = (bf16[16,2560]{1,0:T(8,128)(2,1)S(1)}, bf16[16,2560]{1,0:T(8,128)(2,1)}, u32[]{:S(2)}) copy-start(bf16[16,2560]{1,0:T(8,128)(2,1)} %param.15) | copy-start | bytes 245764
  21.0 45.6 %copy-start.7 = (bf16[16,256]{1,0:T(8,128)(2,1)S(1)}, bf16[16,256]{1,0:T(8,128)(2,1)}, u32[]{:S(2)}) copy-start(bf16[16,256]{1,0:T(8,128)(2,1)} %param.24) | copy-start | bytes 24580
  21.0 45.6 %copy-start.8 = (f32[256]{0:T(256)S(1)}, f32[256]{0:T(256)}, u32[]{:S(2)}) copy-start(f32[256]{0:T(256)} %param.25) | copy-start | bytes 3076
  22.3 210.0 %all-to-all-start = ((bf16[128,16,256]{2,1,0:T(8,128)(2,1)}), bf16[128,16,256]{2,1,0:T(8,128)(2,1)S(1)}, u32[]{:S(2)}, u32[]{:S(2)}) async-start(bf16[128,16,256]{2,1,0:T(8,128)(2,1)} %broadcast_select_fusion), calls=%async_computation | async-start | bytes 2097152 | tf_op jit(solution)/shard_map/all_to_all | solution.py:34
  237.2 1.8 copy-start.2
  237.2 1.9 copy-start.3
  239.6 0.7 copy-start.10
Sparse Core Ops, SparseCore 0:
  12.0 201.0 all-reduce.2
Sparse Core Ops, SparseCore 1:
  14.4 69.8 all-gather.1
